TPU v7x, 32 devices: a whole 2x2x4 slice. The times are simulated.
32 devices in a mesh: dp: 8 (over y, x, core), eshard: 4 (over z).
Axes of the slice: x: 2, y: 2, z: 4, core: 2. Of those that a mesh axis runs over, the one named last changes fastest.
Arguments:
- tokens: bfloat16 [2048, 4096], P('dp', 'eshard'), may hold values from -6 to 6
- cotangent: bfloat16 [2048, 4096], P('dp', 'eshard'), may hold values from -6 to 6
- route_ids: int32 [2048, 2], P('dp'), may hold values from 0 to 63, all different within a row; in each aligned block of 256 rows (0 to 255, 256 to 511, ...) at most 16 rows name the same one
- gate_fixed: int32 [2048, 2], P('dp'), may hold values from 1 to 65535
- w_gate: bfloat16 [4096, 32768], P('eshard', 'dp'), may hold values from -0.09375 to 0.09375
- w_up: bfloat16 [4096, 32768], P('eshard', 'dp'), may hold values from -0.09375 to 0.09375
- w_down: bfloat16 [32768, 4096], P('dp', 'eshard'), may hold values from -0.0625 to 0.0625
Outputs:
- mixed: bfloat16 [2048, 4096], P('dp', 'eshard')
- token_grad: bfloat16 [2048, 4096], P('dp', 'eshard')
- grad_w_gate: bfloat16 [4096, 32768], P('eshard', 'dp')
- grad_w_up: bfloat16 [4096, 32768], P('eshard', 'dp')
- grad_w_down: bfloat16 [32768, 4096], P('dp', 'eshard')
Inputs may be any that keep to these rules, and one draw needn't show every extreme that they name: `route_ids`: the two ids of a token differ; among the 256 tokens of one index of dp, no id is named by more than 16 routes, a bound that some block reaches.
All inputs are finite; a program needn't handle non-finite values.
Results may differ from a plain program's by a relative error of at most 0.028.
Values may be sent and summed in bfloat16 or wider, within the bound.
A program may use at most 128 MiB of HBM per device.

v0:
```python
import functools

import jax
import jax.numpy as jnp
from jax import lax
from jax.experimental import pallas as pl
from jax.experimental.pallas import tpu as pltpu
from jax.sharding import PartitionSpec as P

EXPERTS = 4
CAP = 16
WIDTH = 256
VMEM_BYTES = 46 * 1024 * 1024
GRAD_BYTES = 24 * 1024 * 1024


MESH = pl.DeviceIdType.MESH


def contract_cols(left, right):
    return lax.dot_general(
        left, right, (((1,), (1,)), ((), ())), preferred_element_type=jnp.float32
    )


def halves(value):
    high = value.astype(jnp.bfloat16)
    return high, (value - high.astype(jnp.float32)).astype(jnp.bfloat16)


def routing(ids, gates, cap):
    tokens = ids.shape[1]
    f32 = jnp.float32
    values = gates.astype(f32) * (1.0 / 65536.0)
    hits, weights = [], []
    for expert in range(EXPERTS):
        named = (ids == expert).astype(f32)
        hits.append(jnp.sum(named, axis=0, keepdims=True))
        weights.append(jnp.sum(named * values, axis=0, keepdims=True))
    hit = jnp.concatenate(hits, axis=0)
    earlier = (
        lax.broadcasted_iota(jnp.int32, (tokens, tokens), 0)
        < lax.broadcasted_iota(jnp.int32, (tokens, tokens), 1)
    ).astype(jnp.bfloat16)
    slots = jnp.dot(hit.astype(jnp.bfloat16), earlier, preferred_element_type=f32)
    places = lax.broadcasted_iota(jnp.int32, (cap, tokens), 0).astype(f32)
    select, weighted = [], []
    for expert in range(EXPERTS):
        here = (places == slots[expert : expert + 1]).astype(f32) * hits[expert]
        select.append(here)
        weighted.append(here * weights[expert])
    return jnp.concatenate(select, axis=0), jnp.concatenate(weighted, axis=0)


def window_kernel(
    size, groups, members, chunks, width,
    cap, ids_ref, gates_ref, tokens_ref, cot_ref, wg_ref, wu_ref, wd_ref,
    hid_ref, gg_ref, ug_ref, xt_ref, g_ref, back_ref, pick_ref,
    tok_ref, grd_ref, x_ref, wg_v, wu_v, wd_v, x_v, g_v, part, outer, inner, full, out_acc, back_acc, y_send, y_recv,
    w_sem, xs_sem, xr_sem, in_sem, outer_sem, inner_sem, out_sem, ys_sem, yr_sem,
):
    me, z = lax.axis_index("dp"), lax.axis_index("eshard")
    feats = tok_ref.shape[1]
    rows = groups * cap
    half = size // 2
    left = z < half
    middle = jnp.logical_or(z == half - 1, z == half)
    tip = jnp.logical_or(z == 0, z == size - 1)
    inward = jnp.where(left, z + 1, z - 1)
    outward = jnp.where(tip, z, jnp.where(left, z - 1, z + 1))
    distance = jnp.where(left, half - 1 - z, z - half)

    def weight_copies(c):
        cols = pl.ds(pl.multiple_of(c * width, width), width)
        return (
            pltpu.make_async_copy(wg_ref.at[:, cols], wg_v.at[c], w_sem.at[c, 0]),
            pltpu.make_async_copy(wu_ref.at[:, cols], wu_v.at[c], w_sem.at[c, 1]),
            pltpu.make_async_copy(wd_ref.at[cols, :], wd_v.at[c], w_sem.at[c, 2]),
        )

    @pl.loop(0, chunks)
    def _(c):
        for copy in weight_copies(c):
            copy.start()

    barrier = pltpu.get_barrier_semaphore()

    @pl.loop(1, groups)
    def _(k):
        pl.semaphore_signal(
            barrier, inc=1, device_id={"dp": lax.rem(me + k, groups)}, device_id_type=MESH
        )

    pl.semaphore_signal(barrier, inc=1, device_id={"eshard": inward}, device_id_type=MESH)

    @pl.when(jnp.logical_not(tip))
    def _():
        pl.semaphore_signal(barrier, inc=1, device_id={"eshard": outward}, device_id_type=MESH)

    select, weighted = routing(ids_ref[...], gates_ref[...], cap)
    tok_ref[...] = jnp.dot(
        select.astype(jnp.bfloat16), tokens_ref[...], preferred_element_type=jnp.float32
    ).astype(jnp.bfloat16)

    pl.semaphore_wait(barrier, groups + jnp.where(tip, 0, 1))

    def row_copy(src, dst, which, k):
        to = lax.rem(me + k, groups)
        first = pl.multiple_of((to // members) * cap, cap)
        return pltpu.make_async_remote_copy(
            src_ref=src.at[pl.ds(first, cap), :],
            dst_ref=dst.at[me],
            send_sem=xs_sem.at[which, k],
            recv_sem=xr_sem.at[which, k],
            device_id={"dp": to},
            device_id_type=MESH,
        )

    def send_rows(which, src, dst):
        @pl.loop(1, groups)
        def _(k):
            row_copy(src, dst, which, k).start()

        own = pl.multiple_of((me // members) * cap, cap)
        dst[me] = src[pl.ds(own, cap), :]

    def take_rows(which, src, dst):
        @pl.loop(1, groups)
        def _(k):
            row_copy(src, dst, which, k).wait()

    send_rows(0, tok_ref, x_v)
    high, low = halves(weighted)
    grd_ref[...] = (
        jnp.dot(high, cot_ref[...], preferred_element_type=jnp.float32)
        + jnp.dot(low, cot_ref[...], preferred_element_type=jnp.float32)
    ).astype(jnp.bfloat16)
    send_rows(1, grd_ref, g_v)
    pick_ref[0] = jnp.transpose(select).astype(jnp.bfloat16)
    high, low = halves(jnp.transpose(weighted))
    pick_ref[1] = high
    pick_ref[2] = low
    out_acc[...] = jnp.zeros_like(out_acc)
    back_acc[...] = jnp.zeros_like(back_acc)

    take_rows(0, tok_ref, x_v)
    x_ref[...] = x_v[...].reshape(rows, feats)

    def to_outer(c, k):
        return pltpu.make_async_remote_copy(
            src_ref=part.at[c, k], dst_ref=outer.at[c, k],
            send_sem=in_sem.at[c, k], recv_sem=outer_sem.at[c, k],
            device_id={"eshard": inward}, device_id_type=MESH,
        )

    def to_partner(c, k):
        return pltpu.make_async_remote_copy(
            src_ref=part.at[c, k], dst_ref=inner.at[c, k],
            send_sem=in_sem.at[c, k], recv_sem=inner_sem.at[c, k],
            device_id={"eshard": inward}, device_id_type=MESH,
        )

    def sum_out(c, k):
        return pltpu.make_async_remote_copy(
            src_ref=full.at[c, k], dst_ref=inner.at[c, k],
            send_sem=out_sem.at[c, k], recv_sem=inner_sem.at[c, k],
            device_id={"eshard": outward}, device_id_type=MESH,
        )

    def pass_out(c, k):
        return pltpu.make_async_remote_copy(
            src_ref=inner.at[c, k], dst_ref=inner.at[c, k],
            send_sem=out_sem.at[c, k], recv_sem=inner_sem.at[c, k],
            device_id={"eshard": outward}, device_id_type=MESH,
        )

    def forward(c, k):
        to_partner(c, k).wait_recv()
        full[c, k] = (
            part[c, k].astype(jnp.float32) + inner[c, k].astype(jnp.float32)
        ).astype(jnp.bfloat16)

        @pl.when(jnp.logical_not(tip))
        def _():
            sum_out(c, k).start()

    def gather_in(c):
        for copy in weight_copies(c):
            copy.wait()
        for k in range(3):
            if k == 0:
                own = jnp.dot(x_ref[...], wg_v[c], preferred_element_type=jnp.float32)
            elif k == 1:
                own = jnp.dot(x_ref[...], wu_v[c], preferred_element_type=jnp.float32)
            else:

                @pl.when(c == 0)
                def _():
                    take_rows(1, grd_ref, g_v)
                    g_ref[...] = g_v[...].reshape(rows, feats)

                own = contract_cols(g_ref[...], wd_v[c])

            @pl.when(tip)
            def _():
                part[c, k] = own.astype(jnp.bfloat16)

            @pl.when(jnp.logical_not(tip))
            def _():
                to_outer(c, k).wait_recv()
                part[c, k] = (own + outer[c, k].astype(jnp.float32)).astype(jnp.bfloat16)

            @pl.when(middle)
            def _():
                to_partner(c, k).start()

            @pl.when(jnp.logical_not(middle))
            def _():
                to_outer(c, k).start()

            @pl.when(jnp.logical_and(middle, c > 0))
            def _():
                forward(c - 1, k)

    def return_copy(which, k):
        to = lax.rem(me + k, groups)
        return pltpu.make_async_remote_copy(
            src_ref=y_send.at[which, to], dst_ref=y_recv.at[which, me],
            send_sem=ys_sem.at[which, k], recv_sem=yr_sem.at[which, k],
            device_id={"dp": to}, device_id_type=MESH,
        )

    def send_home(which, total):
        y_send[which] = total[...].astype(jnp.bfloat16).reshape(groups, cap, feats)

        @pl.loop(1, groups)
        def _(k):
            return_copy(which, k).start()

        y_recv[which, me] = y_send[which, me]

    def finish(c):
        def summed(k):
            @pl.when(jnp.logical_not(middle))
            def _():
                to_partner(c, k).wait_recv()

            @pl.when(jnp.logical_not(jnp.logical_or(middle, tip)))
            def _():
                pass_out(c, k).start()

            @pl.when(jnp.logical_and(middle, c == chunks - 1))
            def _():
                forward(c, k)

            mine = part[c, k].astype(jnp.float32)
            return inner[c, k].astype(jnp.float32) + jnp.where(middle, mine, jnp.zeros_like(mine))

        gate, up = summed(0), summed(1)
        logistic = 1.0 / (1.0 + jnp.exp(-gate))
        silu = gate * logistic
        product = silu * up
        hidden = product.astype(jnp.bfloat16)
        cols = pl.ds(pl.multiple_of(c * width, width), width)
        out_acc[...] += jnp.dot(hidden, wd_v[c], preferred_element_type=jnp.float32)

        @pl.when(c == chunks - 1)
        def _():
            send_home(0, out_acc)

        down = summed(2)
        gate_grad = (down * up * logistic * (1.0 + gate * (1.0 - logistic))).astype(jnp.bfloat16)
        up_grad = (down * silu).astype(jnp.bfloat16)
        back_acc[...] += contract_cols(gate_grad, wg_v[c]) + contract_cols(up_grad, wu_v[c])

        @pl.when(c == chunks - 1)
        def _():
            send_home(1, back_acc)

        gg_ref[:, cols] = gate_grad
        ug_ref[:, cols] = up_grad
        hid_ref[cols, :] = jnp.transpose(product).astype(jnp.bfloat16)

    lag = jnp.where(middle, 1, 1 + 4 * distance)

    @pl.loop(0, chunks + 1 + 4 * (half - 1))
    def _(t):
        @pl.when(t < chunks)
        def _():
            gather_in(t)

        @pl.when(jnp.logical_and(t >= lag, t - lag < chunks))
        def _():
            finish(t - lag)

        @pl.when(t == 1)
        def _():
            xt_ref[...] = jnp.transpose(x_ref[...].astype(jnp.float32)).astype(jnp.bfloat16)

    @pl.loop(0, chunks)
    def _(c):
        for k in range(3):
            to_outer(c, k).wait_send()

            @pl.when(jnp.logical_not(tip))
            def _():
                sum_out(c, k).wait_send()

    for which in range(2):

        @pl.loop(1, groups)
        def _(k):
            return_copy(which, k).wait()

    back_ref[...] = y_recv[...]


def run_window(ids, gates, tokens, cotangent, w_gate, w_up, w_down):
    groups, size = lax.axis_size("dp"), lax.axis_size("eshard")
    members = groups // EXPERTS
    feats, hidden = w_gate.shape
    cap, count = CAP, tokens.shape[0]
    rows = groups * cap
    width = min(WIDTH, hidden)
    chunks = hidden // width
    bf16, f32 = jnp.bfloat16, jnp.float32
    vmem, hbm = pl.BlockSpec(memory_space=pltpu.VMEM), pl.BlockSpec(memory_space=pl.ANY)
    dma = pltpu.SemaphoreType.DMA
    wide = jax.ShapeDtypeStruct((rows, hidden), bf16)
    stage = pltpu.VMEM((chunks, 3, rows, width), bf16)
    return pl.pallas_call(
        functools.partial(window_kernel, size, groups, members, chunks, width, cap),
        out_shape=(
            jax.ShapeDtypeStruct((hidden, rows), bf16), wide, wide,
            jax.ShapeDtypeStruct((feats, rows), bf16),
            jax.ShapeDtypeStruct((rows, feats), bf16),
            jax.ShapeDtypeStruct((2, groups, cap, feats), bf16),
            jax.ShapeDtypeStruct((3, count, EXPERTS * cap), bf16),
        ),
        in_specs=[vmem, vmem, vmem, vmem, hbm, hbm, hbm],
        out_specs=(vmem,) * 7,
        scratch_shapes=[
            pltpu.VMEM((EXPERTS * cap, feats), bf16),
            pltpu.VMEM((EXPERTS * cap, feats), bf16),
            pltpu.VMEM((rows, feats), bf16),
            pltpu.VMEM((chunks, feats, width), bf16),
            pltpu.VMEM((chunks, feats, width), bf16),
            pltpu.VMEM((chunks, width, feats), bf16),
            pltpu.VMEM((groups, cap, feats), bf16),
            pltpu.VMEM((groups, cap, feats), bf16),
            stage, stage, stage, stage,
            pltpu.VMEM((rows, feats), f32),
            pltpu.VMEM((rows, feats), f32),
            pltpu.VMEM((2, groups, cap, feats), bf16),
            pltpu.VMEM((2, groups, cap, feats), bf16),
            dma((chunks, 3)),
            dma((2, groups)), dma((2, groups)),
            dma((chunks, 3)), dma((chunks, 3)), dma((chunks, 3)), dma((chunks, 3)),
            dma((2, groups)), dma((2, groups)),
        ],
        compiler_params=pltpu.CompilerParams(
            collective_id=0, has_side_effects=True, vmem_limit_bytes=VMEM_BYTES
        ),
    )(ids, gates, tokens, cotangent, w_gate, w_up, w_down)


def gradient_kernel(
    members, xt_ref, gg_ref, ug_ref, hid_ref, g_ref, back_ref, pick_ref,
    mixed_ref, token_ref, gate_ref, up_ref, down_ref,
):
    f32, bf16 = jnp.float32, jnp.bfloat16

    def product(left, right):
        return jnp.dot(left, right, preferred_element_type=f32)

    gate_ref[...] = product(xt_ref[...], gg_ref[...]).astype(bf16)
    up_ref[...] = product(xt_ref[...], ug_ref[...]).astype(bf16)
    down_ref[...] = product(hid_ref[...], g_ref[...]).astype(bf16)

    @pl.when(pl.program_id(0) == 0)
    def _():
        def gathered(which):
            parts = []
            for expert in range(EXPERTS):
                total = back_ref[which, expert * members].astype(f32)
                for member in range(1, members):
                    total = total + back_ref[which, expert * members + member].astype(f32)
                parts.append(total)
            return halves(jnp.concatenate(parts, axis=0))

        high, low = gathered(0)
        mixed_ref[...] = (
            product(pick_ref[1], high) + product(pick_ref[2], high) + product(pick_ref[1], low)
        ).astype(bf16)
        high, low = gathered(1)
        token_ref[...] = (product(pick_ref[0], high) + product(pick_ref[0], low)).astype(bf16)


def run_gradients(count, hidden_t, gate_grad, up_grad, inputs_t, route_grad, back, pick):
    groups = lax.axis_size("dp")
    feats, rows = inputs_t.shape
    hidden = hidden_t.shape[0]
    cap = back.shape[2]
    width = min(4 * WIDTH, hidden)
    bf16 = jnp.bfloat16

    def whole(shape):
        return pl.BlockSpec(shape, lambda i: (0,) * len(shape))

    across = pl.BlockSpec((rows, width), lambda i: (0, i))
    return pl.pallas_call(
        functools.partial(gradient_kernel, groups // EXPERTS),
        grid=(hidden // width,),
        out_shape=(
            jax.ShapeDtypeStruct((count, feats), bf16),
            jax.ShapeDtypeStruct((count, feats), bf16),
            jax.ShapeDtypeStruct((feats, hidden), bf16),
            jax.ShapeDtypeStruct((feats, hidden), bf16),
            jax.ShapeDtypeStruct((hidden, feats), bf16),
        ),
        in_specs=[
            whole((feats, rows)), across, across,
            pl.BlockSpec((width, rows), lambda i: (i, 0)),
            whole((rows, feats)), whole((2, groups, cap, feats)), whole(pick.shape),
        ],
        out_specs=(
            whole((count, feats)), whole((count, feats)),
            pl.BlockSpec((feats, width), lambda i: (0, i)),
            pl.BlockSpec((feats, width), lambda i: (0, i)),
            pl.BlockSpec((width, feats), lambda i: (i, 0)),
        ),
        compiler_params=pltpu.CompilerParams(vmem_limit_bytes=GRAD_BYTES),
    )(inputs_t, gate_grad, up_grad, hidden_t, route_grad, back, pick)


def on_device(tokens, cotangent, route_ids, gate_fixed, w_gate, w_up, w_down):
    hidden_t, gate_grad, up_grad, inputs_t, route_grad, back, pick = run_window(
        jnp.transpose(route_ids), jnp.transpose(gate_fixed), tokens, cotangent, w_gate, w_up, w_down
    )
    return run_gradients(
        tokens.shape[0], hidden_t, gate_grad, up_grad, inputs_t, route_grad, back, pick
    )


def solution(mesh):
    placed = (
        P("dp", "eshard"),
        P("dp", "eshard"),
        P("dp", None),
        P("dp", None),
        P("eshard", "dp"),
        P("eshard", "dp"),
        P("dp", "eshard"),
    )
    return jax.shard_map(
        on_device,
        mesh=mesh,
        in_specs=placed,
        out_specs=(
            P("dp", "eshard"),
            P("dp", "eshard"),
            P("eshard", "dp"),
            P("eshard", "dp"),
            P("dp", "eshard"),
        ),
        check_vma=False,
    )
```

profile of v0, /device:TPU:0, one launch (start us, length us, event | category | flops | bytes accessed | tf_op | source)
XLA Modules:
  0.0 112.4 jit_solution(17150980349333036936)
XLA Ops:
  0.6 0.0 copy-start
  0.6 1.0 copy-done
  1.7 0.0 copy-start.1
  1.7 1.0 copy-done.1
  2.7 0.0 copy-start.2
  2.7 0.7 copy-done.2
  3.4 0.0 copy-start.3
  3.4 0.7 copy-done.3
  4.1 96.2 %shard_map.110 = (bf16[4096,128]{1,0:T(8,128)(2,1)S(1)}, bf16[128,4096]{1,0:T(8,128)(2,1)S(1)}, bf16[128,4096]{1,0:T(8,128)(2,1)S(1)}, bf16[1024,128]{1,0:T(8,12...) custom-call(s32[2,256]{1,0:T(2,128)S(1)} %bitcast.2, ...), custom_call_target="tpu_custom_call" | custom-call | tf_op jit(solution)/shard_map/pallas_call | solution.py:331
  100.3 12.1 %shard_map.111 = (bf16[256,1024]{1,0:T(8,128)(2,1)}, bf16[256,1024]{1,0:T(8,128)(2,1)}, bf16[1024,4096]{1,0:T(8,128)(2,1)}, bf16[1024,4096]{1,0:T(8,128)(2,1)}, bf16[4096,1024]{1,0:T(8,128)(2,1)}) custom-call(bf16[1024,128]{1,0:T(8,128)(2,1)S(1)} %get-tuple-element.12.xt_ref, bf16[128,4096]{1,0:T(8,128)(2,1)S(1)} %get-tuple-element.13.gg_ref, ...), custom_call_target="tpu_custom_call" | custom-call | tf_op jit(solution)/shard_map/pallas_call | solution.py:411
Async XLA Ops:
  0.6 1.0 copy-start
  1.7 1.0 copy-start.1
  2.7 0.7 copy-start.2
  3.4 0.7 copy-start.3
where the time goes:
time: 113 us; the launch traced here: 112 us
  Pallas kernels  108 us (96%)
  local copies, waits for them, and re-layouts  3.44 us (3%)
    pallas_call x1, Pallas kernels, run_window(): pl.pallas_call(functools.partial(window_kernel, size, groups, members, ch...  96.2 us
    pallas_call x1, Pallas kernels, run_gradients(): pl.pallas_call(functools.partial(gradient_kernel, groups // EXPERTS), gri...  12.1 us
    unnamed x8, local copies, waits for them, and re-layouts  3.44 us

commit v1 on v0

v1 whole, which is shorter than its diff:
```python
import functools

import jax
import jax.numpy as jnp
from jax import lax
from jax.experimental import pallas as pl
from jax.experimental.pallas import tpu as pltpu
from jax.sharding import PartitionSpec as P

EXPERTS = 4
CAP = 16
CORES = 2
WIDTH = 256
SPAN = 4
GRAD_WIDTH = 512
VMEM_BYTES = 48 * 1024 * 1024
GRAD_BYTES = 34 * 1024 * 1024


MESH = pl.DeviceIdType.MESH


def contract_cols(left, right):
    return lax.dot_general(
        left, right, (((1,), (1,)), ((), ())), preferred_element_type=jnp.float32
    )


def halves(value):
    high = value.astype(jnp.bfloat16)
    return high, (value - high.astype(jnp.float32)).astype(jnp.bfloat16)


def routing(ids, gates, cap):
    tokens = ids.shape[1]
    f32 = jnp.float32
    values = gates.astype(f32) * (1.0 / 65536.0)
    hits, weights = [], []
    for expert in range(EXPERTS):
        named = (ids == expert).astype(f32)
        hits.append(jnp.sum(named, axis=0, keepdims=True))
        weights.append(jnp.sum(named * values, axis=0, keepdims=True))
    hit = jnp.concatenate(hits, axis=0)
    earlier = (
        lax.broadcasted_iota(jnp.int32, (tokens, tokens), 0)
        < lax.broadcasted_iota(jnp.int32, (tokens, tokens), 1)
    ).astype(jnp.bfloat16)
    slots = jnp.dot(hit.astype(jnp.bfloat16), earlier, preferred_element_type=f32)
    places = lax.broadcasted_iota(jnp.int32, (cap, tokens), 0).astype(f32)
    select, weighted = [], []
    for expert in range(EXPERTS):
        here = (places == slots[expert : expert + 1]).astype(f32) * hits[expert]
        select.append(here)
        weighted.append(here * weights[expert])
    return jnp.concatenate(select, axis=0), jnp.concatenate(weighted, axis=0)


def window_kernel(
    size, groups, members, chunks, width, cap, span, first,
    ids_ref, gates_ref, tokens_ref, cot_ref, wg_ref, wu_ref, wd_ref,
    hid_ref, gg_ref, ug_ref, xt_ref, g_ref, back_ref, pick_ref,
    ids_v, gates_v, tokens_v, cot_v, tok_ref, grd_ref, wg_v, wu_v, wd_v, x_v, g_v,
    part_t, outer_t, inner_t, full_t, slope_t, silu_t,
    part_w, outer_w, inner_w, full_w, slope_w, silu_w,
    out_acc, back_acc, y_send, y_recv,
    a_sem, w_sem, xs_sem, xr_sem, in_sem, outer_sem, inner_sem, out_sem, ys_sem, yr_sem,
):
    f32, bf16 = jnp.float32, jnp.bfloat16
    me, z = lax.axis_index("dp"), lax.axis_index("eshard")
    chips = groups // CORES
    chip, core = me // CORES, lax.rem(me, CORES)
    feats = tok_ref.shape[1]
    near = CORES * cap
    rows = groups * cap
    wides = chunks // span
    units = chunks + wides
    half = size // 2
    left = z < half
    middle = jnp.logical_or(z == half - 1, z == half)
    tip = jnp.logical_or(z == 0, z == size - 1)
    inward = jnp.where(left, z + 1, z - 1)
    outward = jnp.where(tip, z, jnp.where(left, z - 1, z + 1))
    distance = jnp.where(left, half - 1 - z, z - half)

    small = tuple(
        pltpu.make_async_copy(src, dst, a_sem.at[i])
        for i, (src, dst) in enumerate(
            ((ids_ref, ids_v), (gates_ref, gates_v), (tokens_ref, tokens_v), (cot_ref, cot_v))
        )
    )
    for copy in small:
        copy.start()

    def weight_copy(c, k):
        cols = pl.ds(pl.multiple_of(c * width, width), width)
        if k == 0:
            return pltpu.make_async_copy(wg_ref.at[:, cols], wg_v.at[c], w_sem.at[c, 0])
        if k == 1:
            return pltpu.make_async_copy(wu_ref.at[:, cols], wu_v.at[c], w_sem.at[c, 1])
        return pltpu.make_async_copy(wd_ref.at[cols, :], wd_v.at[c], w_sem.at[c, 2])

    for k in range(3):
        for c in range(span):
            weight_copy(c, k).start()

    barrier = pltpu.get_barrier_semaphore()

    @pl.loop(1, groups)
    def _(k):
        pl.semaphore_signal(
            barrier, inc=1, device_id={"dp": lax.rem(me + k, groups)}, device_id_type=MESH
        )

    pl.semaphore_signal(barrier, inc=1, device_id={"eshard": inward}, device_id_type=MESH)

    @pl.when(jnp.logical_not(tip))
    def _():
        pl.semaphore_signal(barrier, inc=1, device_id={"eshard": outward}, device_id_type=MESH)

    small[0].wait()
    small[1].wait()
    select, weighted = routing(ids_v[...], gates_v[...], cap)
    small[2].wait()
    tok_ref[...] = jnp.dot(
        select.astype(bf16), tokens_v[...], preferred_element_type=f32
    ).astype(bf16)

    pl.semaphore_wait(barrier, groups + jnp.where(tip, 0, 1))

    def device_of(slot):
        return lax.rem(chip + slot // CORES, chips) * CORES + lax.rem(slot, CORES)

    def row_copy(src, dst, which, slot):
        to = device_of(slot)
        there = lax.rem(chips - slot // CORES, chips) * CORES + core
        return pltpu.make_async_remote_copy(
            src_ref=src.at[pl.ds(pl.multiple_of((to // members) * cap, cap), cap), :],
            dst_ref=dst.at[pl.ds(pl.multiple_of(there * cap, cap), cap), :],
            send_sem=xs_sem.at[which, slot],
            recv_sem=xr_sem.at[which, there],
            device_id={"dp": to},
            device_id_type=MESH,
        )

    def row_take(src, dst, which, slot):
        pltpu.make_async_remote_copy(
            src_ref=src.at[pl.ds(0, cap), :],
            dst_ref=dst.at[pl.ds(pl.multiple_of(slot * cap, cap), cap), :],
            send_sem=xs_sem.at[which, slot],
            recv_sem=xr_sem.at[which, slot],
            device_id={"dp": device_of(slot)},
            device_id_type=MESH,
        ).wait_recv()

    def send_near(which, src, dst):
        row_copy(src, dst, which, 1 - core).start()
        own = pl.multiple_of((me // members) * cap, cap)
        dst[pl.ds(pl.multiple_of(core * cap, cap), cap), :] = src[pl.ds(own, cap), :]

    def send_far(which, src, dst):
        @pl.loop(CORES, groups)
        def _(slot):
            row_copy(src, dst, which, slot).start()

    def take_far(which, src, dst):
        @pl.loop(CORES, groups)
        def _(slot):
            row_take(src, dst, which, slot)

    send_near(0, tok_ref, x_v)
    high, low = halves(weighted)
    small[3].wait()
    grd_ref[...] = (
        jnp.dot(high, cot_v[...], preferred_element_type=f32)
        + jnp.dot(low, cot_v[...], preferred_element_type=f32)
    ).astype(bf16)
    send_near(1, grd_ref, g_v)
    send_far(0, tok_ref, x_v)
    send_far(1, grd_ref, g_v)

    @pl.loop(span, chunks)
    def _(c):
        for k in range(3):
            weight_copy(c, k).start()

    pick_ref[0] = jnp.transpose(select).astype(bf16)
    high, low = halves(jnp.transpose(weighted))
    pick_ref[1] = high
    pick_ref[2] = low
    out_acc[...] = jnp.zeros_like(out_acc)
    back_acc[...] = jnp.zeros_like(back_acc)

    class Kind:
        def __init__(self, part, outer, inner, full, slope, silu, r0, r1, parts):
            self.part, self.outer, self.inner, self.full = part, outer, inner, full
            self.slope, self.silu = slope, silu
            self.r0, self.r1, self.parts = r0, r1, parts

        def send(self, src, dst, i, t, k, sent, got, to):
            return pltpu.make_async_remote_copy(
                src_ref=src.at[i, k], dst_ref=dst.at[i, k],
                send_sem=sent.at[t, k], recv_sem=got.at[t, k],
                device_id={"eshard": to}, device_id_type=MESH,
            )

        def to_outer(self, i, t, k):
            return self.send(self.part, self.outer, i, t, k, in_sem, outer_sem, inward)

        def to_partner(self, i, t, k):
            return self.send(self.part, self.inner, i, t, k, in_sem, inner_sem, inward)

        def sum_out(self, i, t, k):
            return self.send(self.full, self.inner, i, t, k, out_sem, inner_sem, outward)

        def pass_out(self, i, t, k):
            return self.send(self.inner, self.inner, i, t, k, out_sem, inner_sem, outward)

        def columns(self, j):
            return pl.ds(j * width, width)

        def forward(self, i, t, k):
            self.to_partner(i, t, k).wait_recv()
            self.full[i, k] = (
                self.part[i, k].astype(f32) + self.inner[i, k].astype(f32)
            ).astype(bf16)

            @pl.when(jnp.logical_not(tip))
            def _():
                self.sum_out(i, t, k).start()

        def gather(self, i, t, k):
            own = []
            for j in range(self.parts):
                c = i * self.parts + j
                if k == 0:
                    value = jnp.dot(x_v[self.r0 : self.r1, :], wg_v[c], preferred_element_type=f32)
                elif k == 1:
                    value = jnp.dot(x_v[self.r0 : self.r1, :], wu_v[c], preferred_element_type=f32)
                else:
                    value = contract_cols(g_v[self.r0 : self.r1, :], wd_v[c])
                own.append(value)

            @pl.when(tip)
            def _():
                for j, value in enumerate(own):
                    self.part[i, k, :, self.columns(j)] = value.astype(bf16)

            @pl.when(jnp.logical_not(tip))
            def _():
                self.to_outer(i, t, k).wait_recv()
                for j, value in enumerate(own):
                    self.part[i, k, :, self.columns(j)] = (
                        value + self.outer[i, k, :, self.columns(j)].astype(f32)
                    ).astype(bf16)

            @pl.when(middle)
            def _():
                self.to_partner(i, t, k).start()

            @pl.when(jnp.logical_not(middle))
            def _():
                self.to_outer(i, t, k).start()

        def arrive(self, i, t, k):
            @pl.when(jnp.logical_not(middle))
            def _():
                self.to_partner(i, t, k).wait_recv()

            @pl.when(jnp.logical_not(jnp.logical_or(middle, tip)))
            def _():
                self.pass_out(i, t, k).start()

        def total(self, i, k, j):
            mine = self.part[i, k, :, self.columns(j)].astype(f32)
            return self.inner[i, k, :, self.columns(j)].astype(f32) + jnp.where(
                middle, mine, jnp.zeros_like(mine)
            )

        def activate(self, i, t):
            self.arrive(i, t, 0)
            self.arrive(i, t, 1)
            added = None
            for j in range(self.parts):
                c = i * self.parts + j
                gate, up = self.total(i, 0, j), self.total(i, 1, j)
                logistic = 1.0 / (1.0 + jnp.exp(-gate))
                silu = gate * logistic
                product = silu * up
                self.slope[:, self.columns(j)] = up * logistic * (1.0 + gate * (1.0 - logistic))
                self.silu[:, self.columns(j)] = silu
                term = jnp.dot(product.astype(bf16), wd_v[c], preferred_element_type=f32)
                added = term if added is None else added + term
                cols = pl.ds(pl.multiple_of(c * width, width), width)
                if self.r0:
                    product = jnp.concatenate(
                        (jnp.zeros((self.r0, width), f32), product), axis=0
                    )
                hid_ref[cols, self.r0 : self.r1] = jnp.transpose(product)[:, self.r0 :].astype(bf16)
            out_acc[self.r0 : self.r1, :] += added

        def differentiate(self, i, t):
            self.arrive(i, t, 2)
            added = None
            for j in range(self.parts):
                c = i * self.parts + j
                down = self.total(i, 2, j)
                gate_grad = (down * self.slope[:, self.columns(j)]).astype(bf16)
                up_grad = (down * self.silu[:, self.columns(j)]).astype(bf16)
                term = contract_cols(gate_grad, wg_v[c]) + contract_cols(up_grad, wu_v[c])
                added = term if added is None else added + term
                cols = pl.ds(pl.multiple_of(c * width, width), width)
                gg_ref[self.r0 : self.r1, cols] = gate_grad
                ug_ref[self.r0 : self.r1, cols] = up_grad
            back_acc[self.r0 : self.r1, :] += added

        def drain(self, i, t):
            for k in range(3):
                self.to_outer(i, t, k).wait_send()

                @pl.when(jnp.logical_not(tip))
                def _():
                    self.sum_out(i, t, k).wait_send()

    tall = Kind(part_t, outer_t, inner_t, full_t, slope_t, silu_t, near, rows, 1)
    wide = Kind(part_w, outer_w, inner_w, full_w, slope_w, silu_w, 0, near, span)

    def return_copy(which, slot):
        to = device_of(slot)
        return pltpu.make_async_remote_copy(
            src_ref=y_send.at[which, slot], dst_ref=y_recv.at[which, me],
            send_sem=ys_sem.at[which, slot],
            recv_sem=yr_sem.at[which, me],
            device_id={"dp": to}, device_id_type=MESH,
        )

    def return_take(which, slot):
        source = device_of(slot)
        pltpu.make_async_remote_copy(
            src_ref=y_send.at[which, slot], dst_ref=y_recv.at[which, source],
            send_sem=ys_sem.at[which, slot],
            recv_sem=yr_sem.at[which, source],
            device_id={"dp": source}, device_id_type=MESH,
        ).wait()

    def home_far(which, acc):
        y_send[which, CORES:] = acc[near:, :].astype(bf16).reshape(groups - CORES, cap, feats)

        @pl.loop(CORES, groups)
        def _(slot):
            return_copy(which, slot).start()

    def home_near(which, acc):
        y_send[which, :CORES] = acc[:near, :].astype(bf16).reshape(CORES, cap, feats)
        return_copy(which, 1 - core).start()
        y_recv[which, me] = y_send[which, core]

    lag = jnp.where(middle, 2, 2 + 4 * distance)
    late = first + chunks

    def is_wide(t):
        return jnp.logical_and(
            jnp.logical_and(t >= 0, t < units), jnp.logical_or(t < first, t >= late)
        )

    def is_tall(t):
        return jnp.logical_and(t >= first, t < late)

    def wide_index(t):
        return jnp.where(t < first, t, t - chunks)

    def wait_weights(i, parts, k):
        for j in range(parts):
            weight_copy(i * parts + j, k).wait()

    @pl.loop(0, units + 2 + 4 * (half - 1))
    def _(t):
        before, done = t - 1, t - lag
        for k in range(3):

            @pl.when(is_wide(t))
            def _():
                i = wide_index(t)

                @pl.when(t < first)
                def _():
                    wait_weights(i, span, k)

                if k != 1:

                    @pl.when(t == 0)
                    def _():
                        if k == 0:
                            row_take(tok_ref, x_v, 0, 1 - core)
                        else:
                            row_take(grd_ref, g_v, 1, 1 - core)

                wide.gather(i, t, k)

            @pl.when(is_tall(t))
            def _():
                i = t - first

                @pl.when(i >= first * span)
                def _():
                    wait_weights(i, 1, k)

                if k != 1:

                    @pl.when(i == 0)
                    def _():
                        if k == 0:
                            take_far(0, tok_ref, x_v)
                        else:
                            take_far(1, grd_ref, g_v)

                tall.gather(i, t, k)

            @pl.when(middle)
            def _():
                @pl.when(is_wide(before))
                def _():
                    wide.forward(wide_index(before), before, k)

                @pl.when(is_tall(before))
                def _():
                    tall.forward(before - first, before, k)

            if k == 0:

                @pl.when(is_wide(done))
                def _():
                    wide.activate(wide_index(done), done)

                @pl.when(is_tall(done))
                def _():
                    tall.activate(done - first, done)

                @pl.when(done == late - 1)
                def _():
                    home_far(0, out_acc)

                @pl.when(done == units - 1)
                def _():
                    home_near(0, out_acc)

            if k == 1:

                @pl.when(is_wide(done))
                def _():
                    wide.differentiate(wide_index(done), done)

                @pl.when(is_tall(done))
                def _():
                    tall.differentiate(done - first, done)

                @pl.when(done == late - 1)
                def _():
                    home_far(1, back_acc)

                @pl.when(done == units - 1)
                def _():
                    home_near(1, back_acc)

        @pl.when(t == first + 1)
        def _():
            xt_ref[...] = jnp.transpose(x_v[...].astype(f32)).astype(bf16)
            g_ref[...] = g_v[...]

    @pl.loop(0, units)
    def _(t):
        @pl.when(is_wide(t))
        def _():
            wide.drain(wide_index(t), t)

        @pl.when(is_tall(t))
        def _():
            tall.drain(t - first, t)

    for which in range(2):
        row_copy(tok_ref, x_v, which, 1 - core).wait_send()
        return_take(which, 1 - core)

        @pl.loop(CORES, groups)
        def _(slot):
            row_copy(tok_ref, x_v, which, slot).wait_send()
            return_take(which, slot)

    back_ref[...] = y_recv[...]


def run_window(ids, gates, tokens, cotangent, w_gate, w_up, w_down):
    groups, size = lax.axis_size("dp"), lax.axis_size("eshard")
    members = groups // EXPERTS
    feats, hidden = w_gate.shape
    cap, count = CAP, tokens.shape[0]
    rows, near = groups * cap, CORES * cap
    width = min(WIDTH, hidden)
    chunks = hidden // width
    span = SPAN if chunks % (2 * SPAN) == 0 else 1
    wides = chunks // span
    first = wides // 2
    units = chunks + wides
    bf16, f32 = jnp.bfloat16, jnp.float32
    vmem, hbm = pl.BlockSpec(memory_space=pltpu.VMEM), pl.BlockSpec(memory_space=pl.ANY)
    dma = pltpu.SemaphoreType.DMA
    gathered = jax.ShapeDtypeStruct((rows, hidden), bf16)
    tall = pltpu.VMEM((chunks, 3, rows - near, width), bf16)
    wide = pltpu.VMEM((wides, 3, near, span * width), bf16)
    tall_f32 = pltpu.VMEM((rows - near, width), f32)
    wide_f32 = pltpu.VMEM((near, span * width), f32)
    return pl.pallas_call(
        functools.partial(window_kernel, size, groups, members, chunks, width, cap, span, first),
        out_shape=(
            jax.ShapeDtypeStruct((hidden, rows), bf16), gathered, gathered,
            jax.ShapeDtypeStruct((feats, rows), bf16),
            jax.ShapeDtypeStruct((rows, feats), bf16),
            jax.ShapeDtypeStruct((2, groups, cap, feats), bf16),
            jax.ShapeDtypeStruct((3, count, EXPERTS * cap), bf16),
        ),
        in_specs=[hbm] * 7,
        out_specs=(vmem,) * 7,
        scratch_shapes=[
            pltpu.VMEM(ids.shape, jnp.int32),
            pltpu.VMEM(gates.shape, jnp.int32),
            pltpu.VMEM(tokens.shape, bf16),
            pltpu.VMEM(cotangent.shape, bf16),
            pltpu.VMEM((EXPERTS * cap, feats), bf16),
            pltpu.VMEM((EXPERTS * cap, feats), bf16),
            pltpu.VMEM((chunks, feats, width), bf16),
            pltpu.VMEM((chunks, feats, width), bf16),
            pltpu.VMEM((chunks, width, feats), bf16),
            pltpu.VMEM((rows, feats), bf16),
            pltpu.VMEM((rows, feats), bf16),
            tall, tall, tall, tall, tall_f32, tall_f32,
            wide, wide, wide, wide, wide_f32, wide_f32,
            pltpu.VMEM((rows, feats), f32),
            pltpu.VMEM((rows, feats), f32),
            pltpu.VMEM((2, groups, cap, feats), bf16),
            pltpu.VMEM((2, groups, cap, feats), bf16),
            dma((4,)), dma((chunks, 3)),
            dma((2, groups)), dma((2, groups)),
            dma((units, 3)), dma((units, 3)), dma((units, 3)), dma((units, 3)),
            dma((2, groups)), dma((2, groups)),
        ],
        compiler_params=pltpu.CompilerParams(
            collective_id=0, has_side_effects=True, vmem_limit_bytes=VMEM_BYTES
        ),
    )(ids, gates, tokens, cotangent, w_gate, w_up, w_down)


def gradient_kernel(
    members, width, xt_ref, gg_ref, ug_ref, hid_ref, g_ref, back_ref, pick_ref,
    mixed_ref, token_ref, gate_ref, up_ref, down_ref,
    mixed_v, token_v, gate_v, up_v, down_v, row_sem, sem,
):
    f32, bf16 = jnp.float32, jnp.bfloat16

    def product(left, right):
        return jnp.dot(left, right, preferred_element_type=f32)

    def copies(i):
        cols = pl.ds(pl.multiple_of(i * width, width), width)
        return (
            pltpu.make_async_copy(gate_v.at[i], gate_ref.at[:, cols], sem.at[i, 0]),
            pltpu.make_async_copy(up_v.at[i], up_ref.at[:, cols], sem.at[i, 1]),
            pltpu.make_async_copy(down_v.at[i], down_ref.at[cols, :], sem.at[i, 2]),
        )

    blocks = gate_v.shape[0]

    @pl.loop(0, blocks)
    def _(i):
        cols = pl.ds(pl.multiple_of(i * width, width), width)
        gate_copy, up_copy, down_copy = copies(i)
        gate_v[i] = product(xt_ref[...], gg_ref[:, cols]).astype(bf16)
        gate_copy.start()
        up_v[i] = product(xt_ref[...], ug_ref[:, cols]).astype(bf16)
        up_copy.start()
        down_v[i] = product(hid_ref[cols, :], g_ref[...]).astype(bf16)
        down_copy.start()

    def gathered(which):
        parts = []
        for expert in range(EXPERTS):
            total = back_ref[which, expert * members].astype(f32)
            for member in range(1, members):
                total = total + back_ref[which, expert * members + member].astype(f32)
            parts.append(total)
        return halves(jnp.concatenate(parts, axis=0))

    high, low = gathered(0)
    mixed_v[...] = (
        product(pick_ref[1], high) + product(pick_ref[2], high) + product(pick_ref[1], low)
    ).astype(bf16)
    mixed_copy = pltpu.make_async_copy(mixed_v, mixed_ref, row_sem.at[0])
    mixed_copy.start()
    high, low = gathered(1)
    token_v[...] = (product(pick_ref[0], high) + product(pick_ref[0], low)).astype(bf16)
    token_copy = pltpu.make_async_copy(token_v, token_ref, row_sem.at[1])
    token_copy.start()

    @pl.loop(0, blocks)
    def _(i):
        for copy in copies(i):
            copy.wait()

    mixed_copy.wait()
    token_copy.wait()


def run_gradients(count, hidden_t, gate_grad, up_grad, inputs_t, route_grad, back, pick):
    groups = lax.axis_size("dp")
    feats = inputs_t.shape[0]
    hidden = hidden_t.shape[0]
    width = min(GRAD_WIDTH, hidden)
    blocks = hidden // width
    bf16 = jnp.bfloat16
    vmem, hbm = pl.BlockSpec(memory_space=pltpu.VMEM), pl.BlockSpec(memory_space=pl.ANY)
    return pl.pallas_call(
        functools.partial(gradient_kernel, groups // EXPERTS, width),
        out_shape=(
            jax.ShapeDtypeStruct((count, feats), bf16),
            jax.ShapeDtypeStruct((count, feats), bf16),
            jax.ShapeDtypeStruct((feats, hidden), bf16),
            jax.ShapeDtypeStruct((feats, hidden), bf16),
            jax.ShapeDtypeStruct((hidden, feats), bf16),
        ),
        in_specs=[vmem] * 7,
        out_specs=(hbm,) * 5,
        scratch_shapes=[
            pltpu.VMEM((count, feats), bf16),
            pltpu.VMEM((count, feats), bf16),
            pltpu.VMEM((blocks, feats, width), bf16),
            pltpu.VMEM((blocks, feats, width), bf16),
            pltpu.VMEM((blocks, width, feats), bf16),
            pltpu.SemaphoreType.DMA((2,)),
            pltpu.SemaphoreType.DMA((blocks, 3)),
        ],
        compiler_params=pltpu.CompilerParams(vmem_limit_bytes=GRAD_BYTES),
    )(inputs_t, gate_grad, up_grad, hidden_t, route_grad, back, pick)


def on_device(tokens, cotangent, route_ids, gate_fixed, w_gate, w_up, w_down):
    hidden_t, gate_grad, up_grad, inputs_t, route_grad, back, pick = run_window(
        *(pltpu.with_memory_space_constraint(a, pltpu.HBM) for a in (jnp.transpose(route_ids), jnp.transpose(gate_fixed), tokens, cotangent)), w_gate, w_up, w_down
    )
    return run_gradients(
        tokens.shape[0], hidden_t, gate_grad, up_grad, inputs_t, route_grad, back, pick
    )


def solution(mesh):
    placed = (
        P("dp", "eshard"),
        P("dp", "eshard"),
        P("dp", None),
        P("dp", None),
        P("eshard", "dp"),
        P("eshard", "dp"),
        P("dp", "eshard"),
    )
    return jax.shard_map(
        on_device,
        mesh=mesh,
        in_specs=placed,
        out_specs=(
            P("dp", "eshard"),
            P("dp", "eshard"),
            P("eshard", "dp"),
            P("eshard", "dp"),
            P("dp", "eshard"),
        ),
        check_vma=False,
    )
```

time: 113 us -> 101 us (0.89)
  Pallas kernels: 108 us -> 100 us
  local copies, waits for them, and re-layouts: 3.44 us -> 0 us
    pallas_call x1, Pallas kernels: 96.2 us -> 90.6 us  [run_window(): pl.pallas_call(functools.partial(window_kernel, size, groups, members, ch...]
    unnamed x8 -> x0, local copies, waits for them, and re-layouts: 3.44 us -> none
    pallas_call x1, Pallas kernels: 12.1 us -> 9.76 us  [run_gradients(): pl.pallas_call(functools.partial(gradient_kernel, groups // EXPERTS, widt...]
where the time goes in v1:
time: 101 us
  Pallas kernels  100 us (99%)
    pallas_call x1, Pallas kernels, run_window(): pl.pallas_call(functools.partial(window_kernel, size, groups, members, ch...  90.6 us
    pallas_call x1, Pallas kernels, run_gradients(): pl.pallas_call(functools.partial(gradient_kernel, groups // EXPERTS, widt...  9.76 us

profile of v1, /device:TPU:0, one launch (start us, length us, event | category | flops | bytes accessed | tf_op | source)
XLA Modules:
  0.0 101.0 jit_solution(13869203458177865485)
XLA Ops:
  0.6 90.6 %shard_map.110 = (bf16[4096,128]{1,0:T(8,128)(2,1)S(1)}, bf16[128,4096]{1,0:T(8,128)(2,1)S(1)}, bf16[128,4096]{1,0:T(8,128)(2,1)S(1)}, bf16[1024,128]{1,0:T(8,12...) custom-call(s32[2,256]{1,0:T(2,128)} %bitcast.2, ...), custom_call_target="tpu_custom_call" | custom-call | tf_op jit(solution)/shard_map/pallas_call | solution.py:511
  91.2 9.8 %shard_map.111 = (bf16[256,1024]{1,0:T(8,128)(2,1)}, bf16[256,1024]{1,0:T(8,128)(2,1)}, bf16[1024,4096]{1,0:T(8,128)(2,1)}, bf16[1024,4096]{1,0:T(8,128)(2,1)}, bf16[4096,1024]{1,0:T(8,128)(2,1)}) custom-call(bf16[1024,128]{1,0:T(8,128)(2,1)S(1)} %get-tuple-element.12.xt_ref, bf16[128,4096]{1,0:T(8,128)(2,1)S(1)} %get-tuple-element.13.gg_ref, ...), custom_call_target="tpu_custom_call" | custom-call | tf_op jit(solution)/shard_map/pallas_call | solution.py:619

commit v2 on v1

--- a/solution.py
+++ b/solution.py
@@ -13,8 +13,9 @@
 WIDTH = 256
 SPAN = 4
 GRAD_WIDTH = 512
-VMEM_BYTES = 48 * 1024 * 1024
-GRAD_BYTES = 34 * 1024 * 1024
+EARLY = 4
+VMEM_BYTES = 43 * 1024 * 1024
+GRAD_BYTES = 27 * 1024 * 1024
 
 
 MESH = pl.DeviceIdType.MESH
@@ -56,12 +57,13 @@
 
 
 def window_kernel(
-    size, groups, members, chunks, width, cap, span, first,
+    size, groups, members, chunks, width, cap, span, early, broad,
     ids_ref, gates_ref, tokens_ref, cot_ref, wg_ref, wu_ref, wd_ref,
-    hid_ref, gg_ref, ug_ref, xt_ref, g_ref, back_ref, pick_ref,
+    hid_ref, gg_ref, ug_ref, xt_ref, g_ref, back_ref, pick_ref, soon_ref,
     ids_v, gates_v, tokens_v, cot_v, tok_ref, grd_ref, wg_v, wu_v, wd_v, x_v, g_v,
     part_t, outer_t, inner_t, full_t, slope_t, silu_t,
     part_w, outer_w, inner_w, full_w, slope_w, silu_w,
+    part_f, outer_f, inner_f, full_f, slope_f, silu_f,
     out_acc, back_acc, y_send, y_recv,
     a_sem, w_sem, xs_sem, xr_sem, in_sem, outer_sem, inner_sem, out_sem, ys_sem, yr_sem,
 ):
@@ -72,8 +74,7 @@
     feats = tok_ref.shape[1]
     near = CORES * cap
     rows = groups * cap
-    wides = chunks // span
-    units = chunks + wides
+    units = chunks + 2
     half = size // 2
     left = z < half
     middle = jnp.logical_or(z == half - 1, z == half)
@@ -228,10 +229,10 @@
             def _():
                 self.sum_out(i, t, k).start()
 
-        def gather(self, i, t, k):
+        def gather(self, i, c0, t, k):
             own = []
             for j in range(self.parts):
-                c = i * self.parts + j
+                c = c0 + j
                 if k == 0:
                     value = jnp.dot(x_v[self.r0 : self.r1, :], wg_v[c], preferred_element_type=f32)
                 elif k == 1:
@@ -276,12 +277,12 @@
                 middle, mine, jnp.zeros_like(mine)
             )
 
-        def activate(self, i, t):
+        def activate(self, i, c0, t):
             self.arrive(i, t, 0)
             self.arrive(i, t, 1)
             added = None
             for j in range(self.parts):
-                c = i * self.parts + j
+                c = c0 + j
                 gate, up = self.total(i, 0, j), self.total(i, 1, j)
                 logistic = 1.0 / (1.0 + jnp.exp(-gate))
                 silu = gate * logistic
@@ -298,11 +299,11 @@
                 hid_ref[cols, self.r0 : self.r1] = jnp.transpose(product)[:, self.r0 :].astype(bf16)
             out_acc[self.r0 : self.r1, :] += added
 
-        def differentiate(self, i, t):
+        def differentiate(self, i, c0, t):
             self.arrive(i, t, 2)
             added = None
             for j in range(self.parts):
-                c = i * self.parts + j
+                c = c0 + j
                 down = self.total(i, 2, j)
                 gate_grad = (down * self.slope[:, self.columns(j)]).astype(bf16)
                 up_grad = (down * self.silu[:, self.columns(j)]).astype(bf16)
@@ -323,6 +324,7 @@
 
     tall = Kind(part_t, outer_t, inner_t, full_t, slope_t, silu_t, near, rows, 1)
     wide = Kind(part_w, outer_w, inner_w, full_w, slope_w, silu_w, 0, near, span)
+    whole = Kind(part_f, outer_f, inner_f, full_f, slope_f, silu_f, 0, rows, 1)
 
     def return_copy(which, slot):
         to = device_of(slot)
@@ -355,126 +357,114 @@
         y_recv[which, me] = y_send[which, core]
 
     lag = jnp.where(middle, 2, 2 + 4 * distance)
-    late = first + chunks
-
-    def is_wide(t):
-        return jnp.logical_and(
-            jnp.logical_and(t >= 0, t < units), jnp.logical_or(t < first, t >= late)
-        )
-
-    def is_tall(t):
-        return jnp.logical_and(t >= first, t < late)
-
-    def wide_index(t):
-        return jnp.where(t < first, t, t - chunks)
-
-    def wait_weights(i, parts, k):
+    last = units - 1
+
+    def each_kind(t, body):
+        @pl.when(jnp.logical_or(t == 0, t == last))
+        def _():
+            body(wide, jnp.where(t == 0, 0, 1), jnp.where(t == 0, 0, chunks - span), t)
+
+        c = t - 1
+        edge = jnp.logical_or(c < span, c >= chunks - span)
+        inside = jnp.logical_and(c >= 0, c < chunks)
+
+        @pl.when(jnp.logical_and(inside, edge))
+        def _():
+            body(tall, jnp.where(c < span, c, c - (chunks - 2 * span)), c, t)
+
+        @pl.when(jnp.logical_and(inside, jnp.logical_not(edge)))
+        def _():
+            body(whole, c - span, c, t)
+
+    def wait_weights(c0, parts, k):
         for j in range(parts):
-            weight_copy(i * parts + j, k).wait()
+            weight_copy(c0 + j, k).wait()
 
     @pl.loop(0, units + 2 + 4 * (half - 1))
     def _(t):
         before, done = t - 1, t - lag
         for k in range(3):
 
-            @pl.when(is_wide(t))
-            def _():
-                i = wide_index(t)
-
-                @pl.when(t < first)
-                def _():
-                    wait_weights(i, span, k)
-
-                if k != 1:
+            def start(kind, i, c0, t):
+                if kind is wide:
 
                     @pl.when(t == 0)
                     def _():
+                        wait_weights(0, span, k)
                         if k == 0:
                             row_take(tok_ref, x_v, 0, 1 - core)
-                        else:
+                        if k == 2:
                             row_take(grd_ref, g_v, 1, 1 - core)
 
-                wide.gather(i, t, k)
-
-            @pl.when(is_tall(t))
-            def _():
-                i = t - first
-
-                @pl.when(i >= first * span)
-                def _():
-                    wait_weights(i, 1, k)
-
-                if k != 1:
-
-                    @pl.when(i == 0)
+                else:
+
+                    @pl.when(c0 >= span)
+                    def _():
+                        wait_weights(c0, 1, k)
+
+                if kind is tall and k != 1:
+
+                    @pl.when(c0 == 0)
                     def _():
                         if k == 0:
                             take_far(0, tok_ref, x_v)
                         else:
                             take_far(1, grd_ref, g_v)
 
-                tall.gather(i, t, k)
+                kind.gather(i, c0, t, k)
+
+            each_kind(t, start)
 
             @pl.when(middle)
             def _():
-                @pl.when(is_wide(before))
-                def _():
-                    wide.forward(wide_index(before), before, k)
-
-                @pl.when(is_tall(before))
-                def _():
-                    tall.forward(before - first, before, k)
+                each_kind(before, lambda kind, i, c0, t: kind.forward(i, t, k))
 
             if k == 0:
-
-                @pl.when(is_wide(done))
-                def _():
-                    wide.activate(wide_index(done), done)
-
-                @pl.when(is_tall(done))
-                def _():
-                    tall.activate(done - first, done)
-
-                @pl.when(done == late - 1)
+                each_kind(done, lambda kind, i, c0, t: kind.activate(i, c0, t))
+
+                @pl.when(done == last - 1)
                 def _():
                     home_far(0, out_acc)
 
-                @pl.when(done == units - 1)
+                @pl.when(done == last)
                 def _():
                     home_near(0, out_acc)
 
             if k == 1:
-
-                @pl.when(is_wide(done))
-                def _():
-                    wide.differentiate(wide_index(done), done)
-
-                @pl.when(is_tall(done))
-                def _():
-                    tall.differentiate(done - first, done)
-
-                @pl.when(done == late - 1)
+                each_kind(done, lambda kind, i, c0, t: kind.differentiate(i, c0, t))
+
+                @pl.when(done == last - 1)
                 def _():
                     home_far(1, back_acc)
 
-                @pl.when(done == units - 1)
+                @pl.when(done == last)
                 def _():
                     home_near(1, back_acc)
 
-        @pl.when(t == first + 1)
+        @pl.when(t == 2)
         def _():
             xt_ref[...] = jnp.transpose(x_v[...].astype(f32)).astype(bf16)
             g_ref[...] = g_v[...]
 
+        per = broad // width
+        for which, source in enumerate((gg_ref, ug_ref)):
+            ready = done - which
+            block = ready // per - 1
+
+            @pl.when(
+                jnp.logical_and(
+                    jnp.logical_and(ready >= per, block < early), lax.rem(ready, per) == 0
+                )
+            )
+            def _():
+                cols = pl.ds(pl.multiple_of(block * broad, broad), broad)
+                soon_ref[which, block] = jnp.dot(
+                    xt_ref[...], source[:, cols], preferred_element_type=f32
+                ).astype(bf16)
+
     @pl.loop(0, units)
     def _(t):
-        @pl.when(is_wide(t))
-        def _():
-            wide.drain(wide_index(t), t)
-
-        @pl.when(is_tall(t))
-        def _():
-            tall.drain(t - first, t)
+        each_kind(t, lambda kind, i, c0, t: kind.drain(i, t))
 
     for which in range(2):
         row_copy(tok_ref, x_v, which, 1 - core).wait_send()
@@ -496,29 +486,32 @@
     rows, near = groups * cap, CORES * cap
     width = min(WIDTH, hidden)
     chunks = hidden // width
-    span = SPAN if chunks % (2 * SPAN) == 0 else 1
-    wides = chunks // span
-    first = wides // 2
-    units = chunks + wides
+    span = max(1, min(SPAN, chunks // 4))
+    units = chunks + 2
+    broad = min(GRAD_WIDTH, hidden)
+    early = max(1, min(EARLY, (chunks - span) // (2 * (broad // width))))
     bf16, f32 = jnp.bfloat16, jnp.float32
     vmem, hbm = pl.BlockSpec(memory_space=pltpu.VMEM), pl.BlockSpec(memory_space=pl.ANY)
     dma = pltpu.SemaphoreType.DMA
     gathered = jax.ShapeDtypeStruct((rows, hidden), bf16)
-    tall = pltpu.VMEM((chunks, 3, rows - near, width), bf16)
-    wide = pltpu.VMEM((wides, 3, near, span * width), bf16)
+    tall = pltpu.VMEM((2 * span, 3, rows - near, width), bf16)
+    wide = pltpu.VMEM((2, 3, near, span * width), bf16)
+    whole = pltpu.VMEM((chunks - 2 * span, 3, rows, width), bf16)
     tall_f32 = pltpu.VMEM((rows - near, width), f32)
     wide_f32 = pltpu.VMEM((near, span * width), f32)
+    whole_f32 = pltpu.VMEM((rows, width), f32)
     return pl.pallas_call(
-        functools.partial(window_kernel, size, groups, members, chunks, width, cap, span, first),
+        functools.partial(window_kernel, size, groups, members, chunks, width, cap, span, early, broad),
         out_shape=(
             jax.ShapeDtypeStruct((hidden, rows), bf16), gathered, gathered,
             jax.ShapeDtypeStruct((feats, rows), bf16),
             jax.ShapeDtypeStruct((rows, feats), bf16),
             jax.ShapeDtypeStruct((2, groups, cap, feats), bf16),
             jax.ShapeDtypeStruct((3, count, EXPERTS * cap), bf16),
+            jax.ShapeDtypeStruct((2, early, feats, broad), bf16),
         ),
         in_specs=[hbm] * 7,
-        out_specs=(vmem,) * 7,
+        out_specs=(vmem,) * 8,
         scratch_shapes=[
             pltpu.VMEM(ids.shape, jnp.int32),
             pltpu.VMEM(gates.shape, jnp.int32),
@@ -533,6 +526,7 @@
             pltpu.VMEM((rows, feats), bf16),
             tall, tall, tall, tall, tall_f32, tall_f32,
             wide, wide, wide, wide, wide_f32, wide_f32,
+            whole, whole, whole, whole, whole_f32, whole_f32,
             pltpu.VMEM((rows, feats), f32),
             pltpu.VMEM((rows, feats), f32),
             pltpu.VMEM((2, groups, cap, feats), bf16),
@@ -549,7 +543,7 @@
 
 
 def gradient_kernel(
-    members, width, xt_ref, gg_ref, ug_ref, hid_ref, g_ref, back_ref, pick_ref,
+    members, width, xt_ref, gg_ref, ug_ref, hid_ref, g_ref, back_ref, pick_ref, soon_ref,
     mixed_ref, token_ref, gate_ref, up_ref, down_ref,
     mixed_v, token_v, gate_v, up_v, down_v, row_sem, sem,
 ):
@@ -558,26 +552,47 @@
     def product(left, right):
         return jnp.dot(left, right, preferred_element_type=f32)
 
-    def copies(i):
-        cols = pl.ds(pl.multiple_of(i * width, width), width)
-        return (
-            pltpu.make_async_copy(gate_v.at[i], gate_ref.at[:, cols], sem.at[i, 0]),
-            pltpu.make_async_copy(up_v.at[i], up_ref.at[:, cols], sem.at[i, 1]),
-            pltpu.make_async_copy(down_v.at[i], down_ref.at[cols, :], sem.at[i, 2]),
+    early = soon_ref.shape[1]
+    blocks = down_v.shape[0]
+
+    def columns(i):
+        return pl.ds(pl.multiple_of(i * width, width), width)
+
+    def soon_copy(which, i):
+        target = gate_ref if which == 0 else up_ref
+        return pltpu.make_async_copy(
+            soon_ref.at[which, i], target.at[:, columns(i)], sem.at[i, which]
         )
 
-    blocks = gate_v.shape[0]
-
-    @pl.loop(0, blocks)
+    def gate_copy(i):
+        return pltpu.make_async_copy(gate_v.at[i - early], gate_ref.at[:, columns(i)], sem.at[i, 0])
+
+    def up_copy(i):
+        return pltpu.make_async_copy(up_v.at[i - early], up_ref.at[:, columns(i)], sem.at[i, 1])
+
+    def down_copy(i):
+        return pltpu.make_async_copy(down_v.at[i], down_ref.at[columns(i), :], sem.at[i, 2])
+
+    def make_down(i):
+        down_v[i] = product(hid_ref[columns(i), :], g_ref[...]).astype(bf16)
+        down_copy(i).start()
+
+    @pl.loop(0, early)
     def _(i):
-        cols = pl.ds(pl.multiple_of(i * width, width), width)
-        gate_copy, up_copy, down_copy = copies(i)
-        gate_v[i] = product(xt_ref[...], gg_ref[:, cols]).astype(bf16)
-        gate_copy.start()
-        up_v[i] = product(xt_ref[...], ug_ref[:, cols]).astype(bf16)
-        up_copy.start()
-        down_v[i] = product(hid_ref[cols, :], g_ref[...]).astype(bf16)
-        down_copy.start()
+        for which in range(2):
+            soon_copy(which, i).start()
+
+    @pl.loop(0, early)
+    def _(i):
+        make_down(i)
+
+    @pl.loop(early, blocks)
+    def _(i):
+        gate_v[i - early] = product(xt_ref[...], gg_ref[:, columns(i)]).astype(bf16)
+        gate_copy(i).start()
+        up_v[i - early] = product(xt_ref[...], ug_ref[:, columns(i)]).astype(bf16)
+        up_copy(i).start()
+        make_down(i)
 
     def gathered(which):
         parts = []
@@ -599,16 +614,23 @@
     token_copy = pltpu.make_async_copy(token_v, token_ref, row_sem.at[1])
     token_copy.start()
 
-    @pl.loop(0, blocks)
+    @pl.loop(0, early)
     def _(i):
-        for copy in copies(i):
-            copy.wait()
+        for which in range(2):
+            soon_copy(which, i).wait()
+        down_copy(i).wait()
+
+    @pl.loop(early, blocks)
+    def _(i):
+        gate_copy(i).wait()
+        up_copy(i).wait()
+        down_copy(i).wait()
 
     mixed_copy.wait()
     token_copy.wait()
 
 
-def run_gradients(count, hidden_t, gate_grad, up_grad, inputs_t, route_grad, back, pick):
+def run_gradients(count, hidden_t, gate_grad, up_grad, inputs_t, route_grad, back, pick, soon):
     groups = lax.axis_size("dp")
     feats = inputs_t.shape[0]
     hidden = hidden_t.shape[0]
@@ -625,27 +647,27 @@
             jax.ShapeDtypeStruct((feats, hidden), bf16),
             jax.ShapeDtypeStruct((hidden, feats), bf16),
         ),
-        in_specs=[vmem] * 7,
+        in_specs=[vmem] * 8,
         out_specs=(hbm,) * 5,
         scratch_shapes=[
             pltpu.VMEM((count, feats), bf16),
             pltpu.VMEM((count, feats), bf16),
-            pltpu.VMEM((blocks, feats, width), bf16),
-            pltpu.VMEM((blocks, feats, width), bf16),
+            pltpu.VMEM((blocks - soon.shape[1], feats, width), bf16),
+            pltpu.VMEM((blocks - soon.shape[1], feats, width), bf16),
             pltpu.VMEM((blocks, width, feats), bf16),
             pltpu.SemaphoreType.DMA((2,)),
             pltpu.SemaphoreType.DMA((blocks, 3)),
         ],
         compiler_params=pltpu.CompilerParams(vmem_limit_bytes=GRAD_BYTES),
-    )(inputs_t, gate_grad, up_grad, hidden_t, route_grad, back, pick)
+    )(inputs_t, gate_grad, up_grad, hidden_t, route_grad, back, pick, soon)
 
 
 def on_device(tokens, cotangent, route_ids, gate_fixed, w_gate, w_up, w_down):
-    hidden_t, gate_grad, up_grad, inputs_t, route_grad, back, pick = run_window(
+    hidden_t, gate_grad, up_grad, inputs_t, route_grad, back, pick, soon = run_window(
         *(pltpu.with_memory_space_constraint(a, pltpu.HBM) for a in (jnp.transpose(route_ids), jnp.transpose(gate_fixed), tokens, cotangent)), w_gate, w_up, w_down
     )
     return run_gradients(
-        tokens.shape[0], hidden_t, gate_grad, up_grad, inputs_t, route_grad, back, pick
+        tokens.shape[0], hidden_t, gate_grad, up_grad, inputs_t, route_grad, back, pick, soon
     )
 
 

time: 101 us -> 99.9 us (0.989)
  no operation moved by 1% of the time
where the time goes in v2:
time: 99.9 us; the launch traced here: 99.7 us
  Pallas kernels  99.1 us (99%)
    pallas_call x1, Pallas kernels, run_window(): pl.pallas_call(functools.partial(window_kernel, size, groups, members, ch...  90.2 us
    pallas_call x1, Pallas kernels, run_gradients(): pl.pallas_call(functools.partial(gradient_kernel, groups // EXPERTS, widt...  8.88 us

profile of v2, /device:TPU:0, one launch (start us, length us, event | category | flops | bytes accessed | tf_op | source)
XLA Modules:
  0.0 99.7 jit_solution(10061542794247160384)
XLA Ops:
  0.6 90.2 %shard_map.110 = (bf16[4096,128]{1,0:T(8,128)(2,1)S(1)}, bf16[128,4096]{1,0:T(8,128)(2,1)S(1)}, bf16[128,4096]{1,0:T(8,128)(2,1)S(1)}, bf16[1024,128]{1,0:T(8,12...) custom-call(s32[2,256]{1,0:T(2,128)} %bitcast.2, ...), custom_call_target="tpu_custom_call" | custom-call | tf_op jit(solution)/shard_map/pallas_call | solution.py:503
  90.9 8.9 %shard_map.111 = (bf16[256,1024]{1,0:T(8,128)(2,1)}, bf16[256,1024]{1,0:T(8,128)(2,1)}, bf16[1024,4096]{1,0:T(8,128)(2,1)}, bf16[1024,4096]{1,0:T(8,128)(2,1)}, bf16[4096,1024]{1,0:T(8,128)(2,1)}) custom-call(bf16[1024,128]{1,0:T(8,128)(2,1)S(1)} %get-tuple-element.13.xt_ref, bf16[128,4096]{1,0:T(8,128)(2,1)S(1)} %get-tuple-element.14.gg_ref, ...), custom_call_target="tpu_custom_call" | custom-call | tf_op jit(solution)/shard_map/pallas_call | solution.py:641

commit v3 on v2

--- a/solution.py
+++ b/solution.py
@@ -179,17 +179,10 @@
     send_far(0, tok_ref, x_v)
     send_far(1, grd_ref, g_v)
 
-    @pl.loop(span, chunks)
-    def _(c):
-        for k in range(3):
-            weight_copy(c, k).start()
-
     pick_ref[0] = jnp.transpose(select).astype(bf16)
     high, low = halves(jnp.transpose(weighted))
     pick_ref[1] = high
     pick_ref[2] = low
-    out_acc[...] = jnp.zeros_like(out_acc)
-    back_acc[...] = jnp.zeros_like(back_acc)
 
     class Kind:
         def __init__(self, part, outer, inner, full, slope, silu, r0, r1, parts):
@@ -440,6 +433,16 @@
                 @pl.when(done == last)
                 def _():
                     home_near(1, back_acc)
+
+        @pl.when(t == 0)
+        def _():
+            @pl.loop(span, chunks)
+            def _(c):
+                for k in range(3):
+                    weight_copy(c, k).start()
+
+            out_acc[...] = jnp.zeros_like(out_acc)
+            back_acc[...] = jnp.zeros_like(back_acc)
 
         @pl.when(t == 2)
         def _():

time: 99.9 us -> 99.9 us (level)
  no operation moved by 1% of the time
where the time goes in v3:
time: 99.9 us; the launch traced here: 99.7 us
  Pallas kernels  99.1 us (99%)
    pallas_call x1, Pallas kernels, run_window(): pl.pallas_call(functools.partial(window_kernel, size, groups, members, ch...  90.2 us
    pallas_call x1, Pallas kernels, run_gradients(): pl.pallas_call(functools.partial(gradient_kernel, groups // EXPERTS, widt...  8.88 us

profile of v3, /device:TPU:0, one launch (start us, length us, event | category | flops | bytes accessed | tf_op | source)
XLA Modules:
  0.0 99.7 jit_solution(3797005968413133639)
XLA Ops:
  0.6 90.2 %shard_map.110 = (bf16[4096,128]{1,0:T(8,128)(2,1)S(1)}, bf16[128,4096]{1,0:T(8,128)(2,1)S(1)}, bf16[128,4096]{1,0:T(8,128)(2,1)S(1)}, bf16[1024,128]{1,0:T(8,12...) custom-call(s32[2,256]{1,0:T(2,128)} %bitcast.2, ...), custom_call_target="tpu_custom_call" | custom-call | tf_op jit(solution)/shard_map/pallas_call | solution.py:506
  90.9 8.9 %shard_map.111 = (bf16[256,1024]{1,0:T(8,128)(2,1)}, bf16[256,1024]{1,0:T(8,128)(2,1)}, bf16[1024,4096]{1,0:T(8,128)(2,1)}, bf16[1024,4096]{1,0:T(8,128)(2,1)}, bf16[4096,1024]{1,0:T(8,128)(2,1)}) custom-call(bf16[1024,128]{1,0:T(8,128)(2,1)S(1)} %get-tuple-element.13.xt_ref, bf16[128,4096]{1,0:T(8,128)(2,1)S(1)} %get-tuple-element.14.gg_ref, ...), custom_call_target="tpu_custom_call" | custom-call | tf_op jit(solution)/shard_map/pallas_call | solution.py:644
